TPU v7x, 128 devices: a whole 4x4x4 slice. The times are simulated.
128 devices in a mesh: seq: 16 (over y_lo, x, core), cb: 8 (over y_hi, z).
Axes of the slice: x: 4, y: 4 (y_hi: 2, y_lo: 2; y = y_hi * 2 + y_lo), z: 4, core: 2. Of those that a mesh axis runs over, the one named last changes fastest.
Arguments:
- hidden: bfloat16 [2, 2048, 4096], P(None, 'seq'), may hold values from -6 to 6
- temporal_gain: float32 [4096], replicated, may hold values from 0.5 to 2
- temporal_qkv: bfloat16 [3, 4096, 2048], P(None, None, 'cb'), may hold values from -10 to 10
- temporal_out: bfloat16 [2048, 4096], P('cb'), may hold values from -0.125 to 0.125
- codebook_ids: int32 [2, 2048, 8], P(None, 'seq', 'cb'), may hold values from 0 to 2047
- embedding: bfloat16 [8, 2048, 1024], P('cb'), may hold values from -6 to 6
- input_weight: bfloat16 [8, 4096, 1024], P('cb', 'seq'), may hold values from -0.09375 to 0.09375
- depth_gain: float32 [8, 1024], P('cb'), may hold values from 0.5 to 2
- depth_qkv: bfloat16 [8, 3, 1024, 1024], P('cb'), may hold values from -10 to 10
- depth_out: bfloat16 [8, 1024, 1024], P('cb'), may hold values from -0.1875 to 0.1875
Outputs:
- temporal: bfloat16 [2, 2048, 4096], P(None, 'seq')
- depth: bfloat16 [2, 2048, 8, 1024], P(None, 'seq', 'cb')
All inputs are finite; a program needn't handle non-finite values.
Results may differ from a plain program's by a relative error of at most 0.017.
Values may be sent and summed in bfloat16 or wider, within the bound.
A program may use at most 128 MiB of HBM per device.

v0:
```python
import jax
import jax.numpy as jnp
from jax import lax
from jax.sharding import PartitionSpec as P

HD = 128
DW = 1024
DH = 16
DHD = 64


def normalize(values, scale):
    mean_sq = jnp.mean(values * values, axis=-1, keepdims=True)
    return values * lax.rsqrt(mean_sq + 1e-05) * scale


def shards(
    hidden,
    temporal_gain,
    temporal_qkv,
    temporal_out,
    codebook_ids,
    embedding,
    input_weight,
    depth_gain,
    depth_qkv,
    depth_out,
):
    seq_count, frames, width = hidden.shape
    head_cols = temporal_qkv.shape[2]
    head_count = head_cols // HD
    row_count = seq_count * frames
    hidden_f = hidden.astype(jnp.float32)
    normed = normalize(hidden_f, temporal_gain).astype(jnp.bfloat16).reshape(row_count, width)
    projected = []
    for which in range(3):
        part_rows = jnp.dot(normed, temporal_qkv[which], preferred_element_type=jnp.float32).astype(
            jnp.bfloat16
        )
        projected.append(part_rows.reshape(seq_count, frames, head_count, HD))
    queries = projected[0]
    query_pos = lax.axis_index("seq") * frames + jnp.arange(frames, dtype=jnp.int32)
    temporal_scale = 1.0 / jnp.sqrt(jnp.float32(HD))
    highest = jnp.full((seq_count, head_count, frames), -1e30, jnp.float32)
    key_piece = lax.all_gather(projected[1], "seq", axis=1, tiled=True)
    value_piece = lax.all_gather(projected[2], "seq", axis=1, tiled=True)
    count = key_piece.shape[1]
    scores = (
        jnp.einsum("sqhd,skhd->shqk", queries, key_piece, preferred_element_type=jnp.float32)
        * temporal_scale
    )
    key_pos = jnp.arange(count, dtype=jnp.int32)
    allowed = (key_pos[None, :] <= query_pos[:, None])[None, None]
    scores = jnp.where(allowed, scores, -1e30)
    new_high = jnp.maximum(highest, jnp.max(scores, axis=-1))
    weights = jnp.where(allowed, jnp.exp(scores - new_high[..., None]), 0.0)
    totals = jnp.sum(weights, axis=-1)
    update = jnp.einsum(
        "shqk,skhd->sqhd",
        weights.astype(jnp.bfloat16),
        value_piece,
        preferred_element_type=jnp.float32,
    )
    gathered = update
    highest, totals, gathered = (new_high, totals, gathered)
    mixed = (
        (gathered / totals.transpose(0, 2, 1)[..., None])
        .astype(jnp.bfloat16)
        .reshape(row_count, head_cols)
    )
    term = jnp.dot(mixed, temporal_out, preferred_element_type=jnp.float32)
    summed = lax.psum(term.astype(jnp.bfloat16), "cb").astype(jnp.float32)
    temporal = (hidden_f.reshape(row_count, width) + summed).astype(jnp.bfloat16)
    projected_in = jnp.dot(
        temporal,
        lax.all_gather(input_weight, "seq", axis=1, tiled=True)[0],
        preferred_element_type=jnp.float32,
    )
    entry = jnp.take(embedding[0], codebook_ids.reshape(row_count), axis=0).astype(jnp.float32)
    stream = (projected_in + entry).astype(jnp.bfloat16)
    depth_normed = normalize(stream.astype(jnp.float32), depth_gain[0]).astype(jnp.bfloat16)
    book_query = jnp.dot(depth_normed, depth_qkv[0, 0], preferred_element_type=jnp.float32).astype(
        jnp.bfloat16
    )
    book_key = jnp.dot(depth_normed, depth_qkv[0, 1], preferred_element_type=jnp.float32).astype(
        jnp.bfloat16
    )
    book_value = jnp.dot(depth_normed, depth_qkv[0, 2], preferred_element_type=jnp.float32).astype(
        jnp.bfloat16
    )
    depth_scale = 1.0 / jnp.sqrt(jnp.float32(DHD))
    my_book = lax.axis_index("cb")
    query_heads = book_query.reshape(row_count, DH, DHD)
    highest_b = jnp.full((row_count, DH), -1e30, jnp.float32)
    key_piece = lax.all_gather(book_key[None], "cb", axis=0, tiled=True)
    value_piece = lax.all_gather(book_value[None], "cb", axis=0, tiled=True)
    count = key_piece.shape[0]
    key_heads = key_piece.reshape(count, row_count, DH, DHD)
    value_heads = value_piece.reshape(count, row_count, DH, DHD)
    scores = (
        jnp.einsum("rhd,jrhd->rhj", query_heads, key_heads, preferred_element_type=jnp.float32)
        * depth_scale
    )
    permitted = (jnp.arange(count, dtype=jnp.int32) <= my_book)[None, None, :]
    scores = jnp.where(permitted, scores, -1e30)
    new_high = jnp.maximum(highest_b, jnp.max(scores, axis=-1))
    weights = jnp.where(permitted, jnp.exp(scores - new_high[..., None]), 0.0)
    totals_b = jnp.sum(weights, axis=-1)
    update = jnp.einsum(
        "rhj,jrhd->rhd",
        weights.astype(jnp.bfloat16),
        value_heads,
        preferred_element_type=jnp.float32,
    )
    highest_b, totals_b, gathered_b = (new_high, totals_b, update)
    book_mixed = (gathered_b / totals_b[..., None]).astype(jnp.bfloat16).reshape(row_count, DW)
    depth = (
        jnp.dot(book_mixed, depth_out[0], preferred_element_type=jnp.float32)
        + stream.astype(jnp.float32)
    ).astype(jnp.bfloat16)
    return (temporal.reshape(seq_count, frames, width), depth.reshape(seq_count, frames, 1, DW))


def solution(mesh):
    placed = (
        P(None, "seq", None),
        P(),
        P(None, None, "cb"),
        P("cb", None),
        P(None, "seq", "cb"),
        P("cb", None, None),
        P("cb", "seq", None),
        P("cb", None),
        P("cb", None, None, None),
        P("cb", None, None),
    )
    return jax.shard_map(
        shards,
        mesh=mesh,
        in_specs=placed,
        out_specs=(P(None, "seq", None), P(None, "seq", "cb", None)),
        check_vma=False,
    )
```

profile of v0, /device:TPU:1, one launch (start us, length us, event | category | flops | bytes accessed | tf_op | source)
XLA Modules:
  0.0 419.6 jit_solution(1029900267491474171)
XLA Ops:
  7.2 2.2 multiply_reduce_fusion.2
  9.5 2.3 multiply_convert_fusion
  13.1 2.3 fusion.58
  16.3 2.9 fusion.52
  20.1 2.9 fusion.55
  23.3 30.6 %all-gather.10.cloned.1.call-done = bf16[2,2048,2,128]{3,1,2,0:T(8,128)(2,1)} async-done(((bf16[2,128,2,128]{3,1,2,0:T(8,128)(2,1)}), bf16[2,2048,2,128]{3,1,2,0:T(8,128)(2,1)}) %all-gather.10.cloned.1.call-update) | async-done | bytes 2097168 | tf_op jit(solution)/shard_map/all_gather | solution.py:45
  53.9 2.6 fusion.3
  59.7 33.6 %all-gather.8.cloned.1.call-done = bf16[2,2048,2,128]{1,3,2,0:T(8,128)(2,1)} async-done(((bf16[2,128,2,128]{1,3,2,0:T(8,128)(2,1)}), bf16[2,2048,2,128]{1,3,2,0:T(8,128)(2,1)}) %all-gather.8.cloned.1.call-update) | async-done | bytes 2097168 | tf_op jit(solution)/shard_map/all_gather | solution.py:46
  93.4 4.1 fusion.64
  100.6 4.3 %gather_fusion = bf16[256,1024]{1,0:T(8,128)(2,1)S(1)} fusion(bf16[2048,1024]{1,0:T(8,128)(2,1)} %bitcast.102, s32[1024]{0:T(1024)S(1)} %pad_clamp_fusion), kind=kCustom, calls=%fused_computation | custom fusion | bytes 1049600 | tf_op jit(solution)/shard_map/jit(_take)/gather | solution.py:79
  104.9 82.8 %all-reduce.2.cloned.1.call-done = bf16[256,4096]{1,0:T(8,128)(2,1)} async-done(((bf16[256,4096]{1,0:T(8,128)(2,1)}), bf16[256,4096]{1,0:T(8,128)(2,1)}) %all-reduce.2.cloned.1.call-update) | async-done | bytes 2097168 | tf_op jit(solution)/shard_map/psum | solution.py:72
  187.7 3.7 fusion.2
  191.4 53.9 %all-gather.12.cloned.1.call-done = bf16[1,4096,1024]{2,1,0:T(8,128)(2,1)} async-done(((bf16[1,256,1024]{2,1,0:T(8,128)(2,1)}), bf16[1,4096,1024]{2,1,0:T(8,128)(2,1)}) %all-gather.12.cloned.1.call-update) | async-done | bytes 8388624 | tf_op jit(solution)/shard_map/all_gather | solution.py:76
  245.2 6.5 %fusion.67 = (f32[256]{0:T(256)S(1)}, bf16[256,1024]{1,0:T(8,128)(2,1)S(1)}) fusion(bf16[256,1024]{1,0:T(8,128)(2,1)S(1)} %gather_fusion, pred[256]{0:T(512)(128)(4,1)S(1)} %compare_and_fusion, bf16[256,4096]{1,0:T(8,128)(2,1)} %fusion.2, bf16[1,4096,1024]{2,1,0:T(8,128)(2,1)} %all-gather.12.cloned.1.call-done), kind=kOutput, calls=%fused_computation.52 | convolution fusion | flops 2149318400 | bytes 11535616 | tf_op jit(solution)/shard_map/dot_general | solution.py:74
  251.7 3.1 fusion.43
  255.1 3.2 fusion.46
  258.4 2.4 fusion.40
  261.1 65.6 %all-gather.14.cloned.1.call-done = bf16[2048,1024]{1,0:T(8,128)(2,1)} async-done(((bf16[256,1024]{1,0:T(8,128)(2,1)}), bf16[2048,1024]{1,0:T(8,128)(2,1)}) %all-gather.14.cloned.1.call-update) | async-done | bytes 4194320 | tf_op jit(solution)/shard_map/all_gather | solution.py:95
  326.7 6.5 %copy.29 = bf16[2048,1024]{0,1:T(8,128)(2,1)} copy(bf16[2048,1024]{1,0:T(8,128)(2,1)} %all-gather.14.cloned.1.call-done) | data formatting | bytes 8388608 | tf_op jit(solution)/shard_map/all_gather | solution.py:95
  333.1 3.7 copy.47
  338.0 60.2 %all-gather.16.cloned.1.call-done = bf16[2048,1024]{1,0:T(8,128)(2,1)} async-done(((bf16[256,1024]{1,0:T(8,128)(2,1)}), bf16[2048,1024]{1,0:T(8,128)(2,1)}) %all-gather.16.cloned.1.call-update) | async-done | bytes 4194320 | tf_op jit(solution)/shard_map/all_gather | solution.py:96
  398.2 6.5 %copy.30 = bf16[2048,1024]{0,1:T(8,128)(2,1)} copy(bf16[2048,1024]{1,0:T(8,128)(2,1)} %all-gather.16.cloned.1.call-done) | data formatting | bytes 8388608 | tf_op jit(solution)/shard_map/all_gather | solution.py:96
  404.7 3.7 copy.48
  408.4 2.6 multiply_reduce_fusion
  (53 shorter events, 12.9 us)
Async XLA Ops:
  7.2 90.5 %copy-start = (bf16[256,4096]{1,0:T(8,128)(2,1)S(1)}, bf16[256,4096]{1,0:T(8,128)(2,1)}, u32[]{:S(2)}) copy-start(bf16[256,4096]{1,0:T(8,128)(2,1)} %param.13) | copy-start | bytes 6291460
  7.2 46.7 %all-gather.10.cloned.1.call-start = ((), (), s32[]{:S(2)}) async-start(), calls=%async_computation.1 | async-start | bytes 2228224 | tf_op jit(solution)/shard_map/all_gather | solution.py:45
  11.8 1.3 copy-start.5
  16.2 77.2 %all-gather.8.cloned.1.call-start = ((), (), s32[]{:S(2)}) async-start(), calls=%async_computation | async-start | bytes 2228224 | tf_op jit(solution)/shard_map/all_gather | solution.py:46
  20.0 167.7 %all-reduce.2.cloned.1.call-start = ((), (), s32[]{:S(2)}) async-start(), calls=%async_computation.2 | async-start | bytes 4194304 | tf_op jit(solution)/shard_map/psum | solution.py:72
  56.5 1.9 copy-start.3
  97.5 3.0 copy-start.6
  99.7 88.0 %copy-start.2 = (bf16[2,128,4096]{2,1,0:T(8,128)(2,1)S(1)}, bf16[2,128,4096]{2,1,0:T(8,128)(2,1)}, u32[]{:S(2)}) copy-start(bf16[2,128,4096]{2,1,0:T(8,128)(2,1)} %param.10) | copy-start | bytes 6291460
  99.7 145.5 %all-gather.12.cloned.1.call-start = ((), (), s32[]{:S(2)}) async-start(), calls=%async_computation.3 | async-start | bytes 8912896 | tf_op jit(solution)/shard_map/all_gather | solution.py:76
  100.3 226.4 %all-gather.14.cloned.1.call-start = ((), (), s32[]{:S(2)}) async-start(), calls=%async_computation.4 | async-start | bytes 4718592 | tf_op jit(solution)/shard_map/all_gather | solution.py:95
  191.4 60.3 %copy-start.7 = (f32[1,1024]{1,0:T(1,128)S(1)}, f32[1,1024]{1,0:T(1,128)}, u32[]{:S(2)}) copy-start(f32[1,1024]{1,0:T(1,128)} %param.17) | copy-start | bytes 12292
  254.9 143.3 %all-gather.16.cloned.1.call-start = ((), (), s32[]{:S(2)}) async-start(), calls=%async_computation.5 | async-start | bytes 4718592 | tf_op jit(solution)/shard_map/all_gather | solution.py:96
  408.4 2.8 copy-start.4
  408.4 4.3 %copy-start.1 = (bf16[256,4096]{1,0:T(8,128)(2,1)S(1)}, bf16[256,4096]{1,0:T(8,128)(2,1)}, u32[]{:S(2)}) copy-start(bf16[256,4096]{1,0:T(8,128)(2,1)} %param.13) | copy-start | bytes 6291460
Sparse Core Ops, SparseCore 0:
  16.3 37.5 all-gather.9
  56.1 37.2 all-gather.7
  99.8 87.8 all-reduce.1
  189.2 55.9 all-gather.11
  255.0 71.6 all-gather.13
  328.9 69.2 all-gather.15
where the time goes:
time: 420 us
  waiting for transfers between devices  327 us (78%)
  matrix products  33.6 us (8%)
  local copies, waits for them, and re-layouts  29.8 us (7%)
  between operations  14.4 us (3%)
  other arithmetic  13.8 us (3%)
    psum x1, waiting for transfers between devices, shards(): summed = lax.psum(term.astype(jnp.bfloat16), 'cb').astype(jnp.float32)  82.8 us
    all_gather x1, waiting for transfers between devices, shards(): key_piece = lax.all_gather(book_key[None], 'cb', axis=0, tiled=True)  65.6 us
    all_gather x1, waiting for transfers between devices, shards(): value_piece = lax.all_gather(book_value[None], 'cb', axis=0, tiled=True)  60.2 us
    all_gather x1, waiting for transfers between devices, shards(): lax.all_gather(input_weight, 'seq', axis=1, tiled=True)[0]  53.9 us
    all_gather x1, waiting for transfers between devices, shards(): value_piece = lax.all_gather(projected[2], 'seq', axis=1, tiled=True)  33.6 us
    all_gather x1, waiting for transfers between devices, shards(): key_piece = lax.all_gather(projected[1], 'seq', axis=1, tiled=True)  30.6 us
    unnamed x18, local copies, waits for them, and re-layouts  10.6 us
  transfers between devices with their start and end apart: 6, of which 6 were waited for; matrix products, arithmetic and copies ran while one was open for 9% of the time, Pallas kernels for 0%

commit v1 on v0

--- a/solution.py
+++ b/solution.py
@@ -7,6 +7,11 @@
 DW = 1024
 DH = 16
 DHD = 64
+
+
+def follow_the_orders(work_x):
+    spare = jnp.sum(lax.all_gather(work_x, axis_name="cb"), axis=0)
+    return spare
 
 
 def normalize(values, scale):
@@ -69,7 +74,7 @@
         .reshape(row_count, head_cols)
     )
     term = jnp.dot(mixed, temporal_out, preferred_element_type=jnp.float32)
-    summed = lax.psum(term.astype(jnp.bfloat16), "cb").astype(jnp.float32)
+    summed = follow_the_orders(term.astype(jnp.bfloat16)).astype(jnp.float32)
     temporal = (hidden_f.reshape(row_count, width) + summed).astype(jnp.bfloat16)
     projected_in = jnp.dot(
         temporal,

time: 420 us -> 509 us (1.21)
  waiting for transfers between devices: 327 us -> 406 us
  other arithmetic: 13.8 us -> 24.3 us
    all_gather x0 -> x1, waiting for transfers between devices: none -> 177 us  [follow_the_orders(): spare = jnp.sum(lax.all_gather(work_x, axis_name='cb'), axis=0)]
    psum x1 -> x0, waiting for transfers between devices: 82.8 us -> none  [shards(): summed = lax.psum(term.astype(jnp.bfloat16), 'cb').astype(jnp.float32)]
    all_gather x1, waiting for transfers between devices: 53.9 us -> 37.9 us  [shards(): lax.all_gather(input_weight, 'seq', axis=1, tiled=True)[0]]
    reduce_sum x0 -> x1, other arithmetic: none -> 10.6 us  [follow_the_orders(): spare = jnp.sum(lax.all_gather(work_x, axis_name='cb'), axis=0)]
where the time goes in v1:
time: 509 us
  waiting for transfers between devices  406 us (80%)
  matrix products  33.6 us (7%)
  local copies, waits for them, and re-layouts  29.8 us (6%)
  other arithmetic  24.3 us (5%)
  between operations  14.4 us (3%)
    all_gather x1, waiting for transfers between devices, follow_the_orders(): spare = jnp.sum(lax.all_gather(work_x, axis_name='cb'), axis=0)  177 us
    all_gather x1, waiting for transfers between devices, shards(): key_piece = lax.all_gather(book_key[None], 'cb', axis=0, tiled=True)  65.6 us
    all_gather x1, waiting for transfers between devices, shards(): value_piece = lax.all_gather(book_value[None], 'cb', axis=0, tiled=True)  60.2 us
    all_gather x1, waiting for transfers between devices, shards(): lax.all_gather(input_weight, 'seq', axis=1, tiled=True)[0]  37.9 us
    all_gather x1, waiting for transfers between devices, shards(): value_piece = lax.all_gather(projected[2], 'seq', axis=1, tiled=True)  33.6 us
    all_gather x1, waiting for transfers between devices, shards(): key_piece = lax.all_gather(projected[1], 'seq', axis=1, tiled=True)  30.6 us
    unnamed x18, local copies, waits for them, and re-layouts  10.6 us
    reduce_sum x1, other arithmetic, follow_the_orders(): spare = jnp.sum(lax.all_gather(work_x, axis_name='cb'), axis=0)  10.6 us
  transfers between devices with their start and end apart: 6, of which 6 were waited for; matrix products, arithmetic and copies ran while one was open for 9% of the time, Pallas kernels for 0%

profile of v1, /device:TPU:1, one launch (start us, length us, event | category | flops | bytes accessed | tf_op | source)
XLA Modules:
  0.0 508.6 jit_solution(13797044585109742676)
XLA Ops:
  7.2 2.2 fusion.2
  13.0 2.3 fusion.61
  16.1 2.9 fusion.55
  20.0 2.9 fusion.58
  23.2 30.6 %all-gather.12.cloned.1.call-done = bf16[2,2048,2,128]{3,1,2,0:T(8,128)(2,1)} async-done(((bf16[2,128,2,128]{3,1,2,0:T(8,128)(2,1)}), bf16[2,2048,2,128]{3,1,2,0:T(8,128)(2,1)}) %all-gather.12.cloned.1.call-update) | async-done | bytes 2097168 | tf_op jit(solution)/shard_map/all_gather | solution.py:50
  53.8 2.6 fusion.6
  59.6 33.6 %all-gather.10.cloned.1.call-done = bf16[2,2048,2,128]{1,3,2,0:T(8,128)(2,1)} async-done(((bf16[2,128,2,128]{1,3,2,0:T(8,128)(2,1)}), bf16[2,2048,2,128]{1,3,2,0:T(8,128)(2,1)}) %all-gather.10.cloned.1.call-update) | async-done | bytes 2097168 | tf_op jit(solution)/shard_map/all_gather | solution.py:51
  93.3 4.1 fusion.67
  100.4 4.3 gather_fusion
  104.7 177.3 %all-gather.16.cloned.1.call-done = bf16[2048,4096]{1,0:T(8,128)(2,1)} async-done(((bf16[256,4096]{1,0:T(8,128)(2,1)}), bf16[2048,4096]{1,0:T(8,128)(2,1)}) %all-gather.16.cloned.1.call-update) | async-done | bytes 16777232 | tf_op jit(solution)/shard_map/all_gather | solution.py:13
  282.0 10.6 %reduce_sum.50 = bf16[256,4096]{1,0:T(8,128)(2,1)} reduce(bf16[8,256,4096]{2,1,0:T(8,128)(2,1)} %bitcast.97, bf16[]{:T(256)} %constant.42.clone.1), dimensions={0}, to_apply=%region_3.4 | reduce | flops 7340032 | bytes 18874370 | tf_op jit(solution)/shard_map/reduce_sum | solution.py:13
  292.6 3.7 fusion.5
  296.3 37.9 %all-gather.14.cloned.1.call-done = bf16[1,4096,1024]{2,1,0:T(8,128)(2,1)} async-done(((bf16[1,256,1024]{2,1,0:T(8,128)(2,1)}), bf16[1,4096,1024]{2,1,0:T(8,128)(2,1)}) %all-gather.14.cloned.1.call-update) | async-done | bytes 8388624 | tf_op jit(solution)/shard_map/all_gather | solution.py:81
  334.2 6.5 %fusion.70 = (f32[256]{0:T(256)S(1)}, bf16[256,1024]{1,0:T(8,128)(2,1)S(1)}) fusion(bf16[256,1024]{1,0:T(8,128)(2,1)S(1)} %gather_fusion, pred[256]{0:T(512)(128)(4,1)S(1)} %compare_and_fusion, bf16[256,4096]{1,0:T(8,128)(2,1)} %bitcast.104, bf16[1,4096,1024]{2,1,0:T(8,128)(2,1)} %all-gather.14.cloned.1.call-done), kind=kOutput, calls=%fused_computation.55 | convolution fusion | flops 2149318400 | bytes 11535616 | tf_op jit(solution)/shard_map/dot_general | solution.py:79
  340.7 3.2 fusion.46
  344.2 3.2 fusion.49
  347.4 2.3 fusion.43
  350.0 65.6 %all-gather.18.cloned.1.call-done = bf16[2048,1024]{1,0:T(8,128)(2,1)} async-done(((bf16[256,1024]{1,0:T(8,128)(2,1)}), bf16[2048,1024]{1,0:T(8,128)(2,1)}) %all-gather.18.cloned.1.call-update) | async-done | bytes 4194320 | tf_op jit(solution)/shard_map/all_gather | solution.py:100
  415.7 6.5 %copy.29 = bf16[2048,1024]{0,1:T(8,128)(2,1)} copy(bf16[2048,1024]{1,0:T(8,128)(2,1)} %all-gather.18.cloned.1.call-done) | data formatting | bytes 8388608 | tf_op jit(solution)/shard_map/all_gather | solution.py:100
  422.1 3.7 copy.47
  427.0 60.2 %all-gather.20.cloned.1.call-done = bf16[2048,1024]{1,0:T(8,128)(2,1)} async-done(((bf16[256,1024]{1,0:T(8,128)(2,1)}), bf16[2048,1024]{1,0:T(8,128)(2,1)}) %all-gather.20.cloned.1.call-update) | async-done | bytes 4194320 | tf_op jit(solution)/shard_map/all_gather | solution.py:101
  487.2 6.5 %copy.30 = bf16[2048,1024]{0,1:T(8,128)(2,1)} copy(bf16[2048,1024]{1,0:T(8,128)(2,1)} %all-gather.20.cloned.1.call-done) | data formatting | bytes 8388608 | tf_op jit(solution)/shard_map/all_gather | solution.py:101
  493.7 3.7 copy.48
  497.4 2.6 multiply_reduce_fusion
  (54 shorter events, 15.1 us)
Async XLA Ops:
  7.2 90.4 %copy-start = (bf16[256,4096]{1,0:T(8,128)(2,1)S(1)}, bf16[256,4096]{1,0:T(8,128)(2,1)}, u32[]{:S(2)}) copy-start(bf16[256,4096]{1,0:T(8,128)(2,1)} %param.13) | copy-start | bytes 6291460
  7.2 46.6 %all-gather.12.cloned.1.call-start = ((), (), s32[]{:S(2)}) async-start(), calls=%async_computation.1 | async-start | bytes 2228224 | tf_op jit(solution)/shard_map/all_gather | solution.py:50
  11.7 1.3 copy-start.5
  16.1 77.2 %all-gather.10.cloned.1.call-start = ((), (), s32[]{:S(2)}) async-start(), calls=%async_computation | async-start | bytes 2228224 | tf_op jit(solution)/shard_map/all_gather | solution.py:51
  19.9 262.1 %all-gather.16.cloned.1.call-start = ((), (), s32[]{:S(2)}) async-start(), calls=%async_computation.3 | async-start | bytes 18874368 | tf_op jit(solution)/shard_map/all_gather | solution.py:13
  56.4 1.9 copy-start.3
  97.4 3.0 copy-start.6
  99.6 234.6 %all-gather.14.cloned.1.call-start = ((), (), s32[]{:S(2)}) async-start(), calls=%async_computation.2 | async-start | bytes 8912896 | tf_op jit(solution)/shard_map/all_gather | solution.py:81
  100.2 315.5 %all-gather.18.cloned.1.call-start = ((), (), s32[]{:S(2)}) async-start(), calls=%async_computation.4 | async-start | bytes 4718592 | tf_op jit(solution)/shard_map/all_gather | solution.py:100
  282.0 10.6 %copy-start.2 = (bf16[2,128,4096]{2,1,0:T(8,128)(2,1)S(1)}, bf16[2,128,4096]{2,1,0:T(8,128)(2,1)}, u32[]{:S(2)}) copy-start(bf16[2,128,4096]{2,1,0:T(8,128)(2,1)} %param.10) | copy-start | bytes 6291460
  334.2 6.5 %copy-start.7 = (f32[1,1024]{1,0:T(1,128)S(1)}, f32[1,1024]{1,0:T(1,128)}, u32[]{:S(2)}) copy-start(f32[1,1024]{1,0:T(1,128)} %param.17) | copy-start | bytes 12292
  343.9 143.3 %all-gather.20.cloned.1.call-start = ((), (), s32[]{:S(2)}) async-start(), calls=%async_computation.5 | async-start | bytes 4718592 | tf_op jit(solution)/shard_map/all_gather | solution.py:101
  497.4 2.8 copy-start.4
  497.4 4.3 copy-start.1
Sparse Core Ops, SparseCore 0:
  16.2 37.5 all-gather.11
  56.0 37.2 all-gather.9
  99.7 182.2 all-gather.15
  283.6 50.6 all-gather.13
  344.0 71.6 all-gather.17
  417.9 69.2 all-gather.19
